TPU v7x, 256 devices: a whole 4x4x8 slice. The times are simulated.
256 devices in a mesh: dp: 32 (over x, z), feat: 8 (over y, core).
Axes of the slice: x: 4, y: 4, z: 8, core: 2. Of those that a mesh axis runs over, the one named last changes fastest.
Arguments:
- hidden_first: bfloat16 [2048, 4096], P('dp', 'feat'), may hold values from -6 to 6
- hidden_second: bfloat16 [2048, 4096], P('dp', 'feat'), may hold values from -11 to 11
- weight: bfloat16 [4096, 8192], P('dp', 'feat'), may hold values from -0.09375 to 0.09375
Outputs:
- total_loss: float32 [], replicated
- grad_weight: bfloat16 [4096, 8192], P('dp', 'feat')
- grad_first: bfloat16 [2048, 4096], P('dp', 'feat')
- grad_second: bfloat16 [2048, 4096], P('dp', 'feat')
All inputs are finite; a program needn't handle non-finite values.
Results may differ from a plain program's by a relative error of at most 0.015.
Values may be sent and summed in bfloat16 or wider, within the bound.
No kernel may reach another device: no remote copies, remote signals or barrier semaphores. Data moves between devices by JAX's collectives and lax.ppermute only.
A program may use at most 64 MiB of HBM per device.

v0:
```python
import jax
import jax.numpy as jnp
from jax import lax
from jax.sharding import PartitionSpec as P


def on_device(hidden_first, hidden_second, weight):
    dp_size = lax.axis_size("dp")
    feat_size = lax.axis_size("feat")
    row_count = hidden_first.shape[0]
    col_count = weight.shape[1]
    total_rows = row_count * dp_size * 1.0
    full_width = col_count * feat_size * 1.0
    full_first, full_second = (
        lax.all_gather(hidden_first, "feat", axis=1, tiled=True),
        lax.all_gather(hidden_second, "feat", axis=1, tiled=True),
    )
    stacked = jnp.concatenate([full_first, full_second], axis=0)
    whole_weight = lax.all_gather(weight, "dp", axis=0, tiled=True)
    outputs = jnp.dot(stacked, whole_weight, preferred_element_type=jnp.float32)
    views = outputs.reshape(2, row_count, col_count)
    col_sum = lax.psum(jnp.sum(views, axis=1), "dp")
    col_mean = col_sum / total_rows
    centered = views - col_mean[:, None, :]
    second_sum = lax.psum(jnp.sum(centered * centered, axis=1), "dp")
    variance = second_sum / (total_rows - 1.0)
    deviation = jnp.sqrt(variance + 0.0001)
    centered_half = centered.astype(jnp.bfloat16)
    gathered = lax.all_gather(centered_half, "dp", axis=1, tiled=True)
    gram_part = jnp.einsum(
        "vrc,vnc->vrn", centered_half, gathered, preferred_element_type=jnp.float32
    )
    gram_rows = lax.psum(gram_part.astype(jnp.bfloat16), "feat").astype(jnp.float32)
    gram_half = gram_rows.astype(jnp.bfloat16)
    spread = jnp.einsum("vrn,vnc->vrc", gram_half, gathered, preferred_element_type=jnp.float32)
    difference = views[0] - views[1]
    local_share = (
        25.0 * jnp.sum(difference * difference) / (total_rows * full_width)
        + 25.0 * jnp.sum(jax.nn.relu(1.0 - deviation)) / (full_width * dp_size)
        + (
            jnp.sum(gram_rows * gram_rows) / ((total_rows - 1.0) ** 2 * feat_size)
            - jnp.sum(variance * variance) / dp_size
        )
        / full_width
    )
    total_loss = lax.psum(local_share, ("dp", "feat"))
    inv_grad = 50.0 / 256.0 * jnp.stack([difference, -difference])
    binding = (deviation < 1.0).astype(jnp.float32)
    hinge_grad = (
        -(25.0 * total_rows / (256.0 * (total_rows - 1.0)))
        * (binding / deviation)[:, None, :]
        * centered
    )
    cov_grad = (
        4.0
        * total_rows
        / 256.0
        * (spread / (total_rows - 1.0) ** 2 - variance[:, None, :] * centered / (total_rows - 1.0))
    )
    grad_views = (inv_grad + hinge_grad + cov_grad).astype(jnp.bfloat16)
    flat_grads = grad_views.reshape(2 * row_count, col_count)
    input_terms = lax.dot_general(
        flat_grads, whole_weight, (((1,), (1,)), ((), ())), preferred_element_type=jnp.float32
    )
    input_grads = lax.psum_scatter(
        input_terms.astype(jnp.bfloat16), "feat", scatter_dimension=1, tiled=True
    )
    grad_first = input_grads[:row_count]
    grad_second = input_grads[row_count:]
    grad_weight = lax.psum_scatter(
        lax.dot_general(
            stacked, flat_grads, (((0,), (0,)), ((), ())), preferred_element_type=jnp.float32
        ).astype(jnp.bfloat16),
        "dp",
        scatter_dimension=0,
        tiled=True,
    )
    return (total_loss, grad_weight, grad_first, grad_second)


def solution(mesh):
    placed = (P("dp", "feat"), P("dp", "feat"), P("dp", "feat"))
    return jax.shard_map(
        on_device,
        mesh=mesh,
        in_specs=placed,
        out_specs=(P(), P("dp", "feat"), P("dp", "feat"), P("dp", "feat")),
        check_vma=False,
    )
```

profile of v0, /device:TPU:8, one launch (start us, length us, event | category | flops | bytes accessed | tf_op | source)
XLA Modules:
  0.0 638.5 jit_solution(8527642386405286671)
XLA Ops:
  7.2 0.7 all-gather.3.cloned.1.call-update
  7.9 0.0 all-gather.5.cloned.1.call-start
  7.9 13.5 %all_gather.12 = bf16[64,4096]{1,0:T(8,128)(2,1)S(1)} all-gather(bf16[64,512]{1,0:T(8,128)(2,1)} %param.3), channel_id=1, replica_groups=mesh['dp'=32,'feat'=8] {'feat'}, dimensions={1}, use_global_device_ids=true | all-gather | bytes 589824 | tf_op jit(solution)/shard_map/all_gather | solution.py:15
  21.5 13.3 %all_gather.13 = bf16[64,4096]{1,0:T(8,128)(2,1)S(1)} all-gather(bf16[64,512]{1,0:T(8,128)(2,1)} %param.4), channel_id=1, replica_groups=mesh['dp'=32,'feat'=8] {'feat'}, dimensions={1}, use_global_device_ids=true | all-gather | bytes 589824 | tf_op jit(solution)/shard_map/all_gather | solution.py:16
  34.9 76.4 %all-gather.3.cloned.1.call-done = bf16[4096,1024]{1,0:T(8,128)(2,1)} async-done(((bf16[128,1024]{1,0:T(8,128)(2,1)}), bf16[4096,1024]{1,0:T(8,128)(2,1)}) %all-gather.3.cloned.1.call-update) | async-done | bytes 8388624 | tf_op jit(solution)/shard_map/all_gather | solution.py:19
  111.3 4.7 bitcast_reduce_fusion
  115.9 72.4 %psum.28 = f32[2,1024]{1,0:T(2,128)S(1)} all-reduce(f32[2,1024]{1,0:T(2,128)S(1)} %get-tuple-element.15), channel_id=1, replica_groups=mesh['dp'=32,'feat'=8] {'dp'}, use_global_device_ids=true, to_apply=%region_2.0 | all-reduce | flops 2048 | bytes 16384 | tf_op jit(solution)/shard_map/psum | solution.py:22
  188.3 0.8 fusion.5
  189.1 0.0 all-reduce.2.cloned.1.call-start
  189.2 72.3 %psum.29 = f32[2,1024]{1,0:T(2,128)S(1)} all-reduce(f32[2,1024]{1,0:T(2,128)S(1)} %get-tuple-element.7), channel_id=1, replica_groups=mesh['dp'=32,'feat'=8] {'dp'}, use_global_device_ids=true, to_apply=%region_4.0 | all-reduce | flops 2048 | bytes 16384 | tf_op jit(solution)/shard_map/psum | solution.py:25
  261.4 19.3 %all-gather.5.cloned.1.call-done = bf16[2,2048,1024]{2,1,0:T(8,128)(2,1)} async-done(((bf16[2,64,1024]{2,1,0:T(8,128)(2,1)}), bf16[2,2048,1024]{2,1,0:T(8,128)(2,1)}) %all-gather.5.cloned.1.call-update) | async-done | bytes 8388624 | tf_op jit(solution)/shard_map/all_gather | solution.py:29
  280.8 6.9 %convolution_convert_fusion.2 = bf16[2,64,2048]{2,1,0:T(8,128)(2,1)} fusion(bf16[2,64,1024]{2,1,0:T(8,128)(2,1)} %get-tuple-element.6, bf16[2,2048,1024]{2,1,0:T(8,128)(2,1)} %all-gather.5.cloned.1.call-done), kind=kOutput, calls=%fused_computation.2 | convolution fusion | flops 537133056 | bytes 9175040 | tf_op jit(solution)/shard_map/vrc,vnc->vrn/dot_general | solution.py:30
  287.8 0.0 reduce-scatter.5.cloned.1.call-start
  287.8 0.6 multiply_reduce_fusion.3
  288.4 0.7 fusion.8
  289.1 59.9 %all-reduce.2.cloned.1.call-done = bf16[2,64,2048]{2,1,0:T(8,128)(2,1)} async-done(((bf16[2,64,2048]{2,1,0:T(8,128)(2,1)}), bf16[2,64,2048]{2,1,0:T(8,128)(2,1)}) %all-reduce.2.cloned.1.call-update) | async-done | bytes 524304 | tf_op jit(solution)/shard_map/psum | solution.py:33
  349.0 5.3 fusion.3
  354.3 7.3 %convolution_convert_fusion.1 = bf16[128,4096]{1,0:T(8,128)(2,1)} fusion(bf16[128,1024]{1,0:T(8,128)(2,1)S(1)} %bitcast.24, bf16[4096,1024]{1,0:T(8,128)(2,1)} %all-gather.3.cloned.1.call-done), kind=kOutput, calls=%fused_computation.1 | convolution fusion | flops 1074266112 | bytes 9699328 | tf_op jit(solution)/shard_map/dot_general | solution.py:62
  361.7 0.0 reduce-scatter.3.cloned.1.call-start
  361.7 5.6 convolution_convert_fusion
  369.3 0.9 multiply_reduce_fusion
  370.8 77.3 %psum.31 = f32[]{:T(128)} all-reduce(f32[]{:T(128)S(6)} %add.33), channel_id=1, replica_groups=mesh['dp'=32,'feat'=8] {'dp','feat'}, use_global_device_ids=true, to_apply=%region_9.10 | all-reduce | flops 1 | bytes 8 | tf_op jit(solution)/shard_map/psum | solution.py:46
  448.2 1.5 fusion.9
  449.7 182.3 %reduce-scatter.3.cloned.1.call-done = bf16[128,1024]{1,0:T(8,128)(2,1)} async-done(((bf16[4096,1024]{1,0:T(8,128)(2,1)}), bf16[128,1024]{1,0:T(8,128)(2,1)}) %reduce-scatter.3.cloned.1.call-update) | async-done | bytes 262160 | tf_op jit(solution)/shard_map/reduce_scatter | solution.py:70
  (11 shorter events, 0.2 us)
Async XLA Ops:
  7.2 104.1 %all-gather.3.cloned.1.call-start = ((), (), s32[]{:S(2)}) async-start(), calls=%async_computation.2 | async-start | bytes 8650752 | tf_op jit(solution)/shard_map/all_gather | solution.py:19
  7.9 272.9 %all-gather.5.cloned.1.call-start = ((), (), s32[]{:S(2)}) async-start(), calls=%async_computation.3 | async-start | bytes 8650752 | tf_op jit(solution)/shard_map/all_gather | solution.py:29
  189.1 159.9 %all-reduce.2.cloned.1.call-start = ((), (), s32[]{:S(2)}) async-start(), calls=%async_computation.4 | async-start | bytes 1048576 | tf_op jit(solution)/shard_map/psum | solution.py:33
  287.8 160.4 %reduce-scatter.5.cloned.1.call-start = ((), (), s32[]{:S(2)}) async-start(), calls=%async_computation.6 | async-start | bytes 1179648 | tf_op jit(solution)/shard_map/reduce_scatter | solution.py:65
  361.7 7.6 %copy-start = (bf16[2,64,2048]{2,1,0:T(8,128)(2,1)S(1)}, bf16[2,64,2048]{2,1,0:T(8,128)(2,1)}, u32[]{:S(2)}) copy-start(bf16[2,64,2048]{2,1,0:T(8,128)(2,1)} %all-reduce.2.cloned.1.call-done) | copy-start | bytes 1572868
  361.7 270.3 %reduce-scatter.3.cloned.1.call-start = ((), (), s32[]{:S(2)}) async-start(), calls=%async_computation.5 | async-start | bytes 8650752 | tf_op jit(solution)/shard_map/reduce_scatter | solution.py:70
Sparse Core Ops, SparseCore 0:
  10.6 100.6 all-gather.2
  189.2 91.5 all-gather.4
  287.9 61.1 all-reduce.1
  361.8 33.2 reduce-scatter.4
  399.5 232.4 reduce-scatter.2
where the time goes:
time: 639 us
  waiting for transfers between devices  339 us (53%)
  blocking collectives  249 us (39%)
  matrix products  29.8 us (5%)
  between operations  16.5 us (3%)
    reduce_scatter x1, waiting for transfers between devices, on_device(): lax.psum_scatter(lax.dot_general(stacked, flat_grads, (((0,), (0,)), ((),...  182 us
    psum x1, blocking collectives, on_device(): total_loss = lax.psum(local_share, ('dp', 'feat'))  77.3 us
    all_gather x1, waiting for transfers between devices, on_device(): whole_weight = lax.all_gather(weight, 'dp', axis=0, tiled=True)  76.4 us
    psum x1, blocking collectives, on_device(): col_sum = lax.psum(jnp.sum(views, axis=1), 'dp')  72.4 us
    psum x1, blocking collectives, on_device(): second_sum = lax.psum(jnp.sum(centered * centered, axis=1), 'dp')  72.3 us
    psum x1, waiting for transfers between devices, on_device(): lax.psum(gram_part.astype(jnp.bfloat16), 'feat').astype(jnp.float32)  59.9 us
    all_gather x1, waiting for transfers between devices, on_device(): gathered = lax.all_gather(centered_half, 'dp', axis=1, tiled=True)  19.3 us
    all_gather x1, blocking collectives, on_device(): lax.all_gather(hidden_first, 'feat', axis=1, tiled=True)  13.5 us
  transfers between devices with their start and end apart: 5, of which 4 were waited for; matrix products, arithmetic and copies ran while one was open for 1% of the time, Pallas kernels for 0%

commit v1 on v0

--- a/solution.py
+++ b/solution.py
@@ -16,7 +16,9 @@
         lax.all_gather(hidden_second, "feat", axis=1, tiled=True),
     )
     stacked = jnp.concatenate([full_first, full_second], axis=0)
-    whole_weight = lax.all_gather(weight, "dp", axis=0, tiled=True)
+    whole_weight = jnp.concatenate(
+        lax.all_to_all(jnp.stack([weight] * lax.axis_size("dp")), "dp", 0, 0), axis=0
+    )
     outputs = jnp.dot(stacked, whole_weight, preferred_element_type=jnp.float32)
     views = outputs.reshape(2, row_count, col_count)
     col_sum = lax.psum(jnp.sum(views, axis=1), "dp")

time: 639 us -> 743 us (1.16)
  waiting for transfers between devices: 339 us -> 424 us
  starting transfers between devices: 0.2 us -> 11.9 us
    all_to_all x0 -> x1, waiting for transfers between devices: none -> 162 us  [on_device(): lax.all_to_all(jnp.stack([weight] * lax.axis_size('dp')), 'dp', 0, 0)]
    all_gather x1 -> x0, waiting for transfers between devices: 76.4 us -> none  [on_device(): whole_weight = lax.all_gather(weight, 'dp', axis=0, tiled=True)]
    all_to_all x0 -> x1, starting transfers between devices: none -> 11.6 us  [on_device(): lax.all_to_all(jnp.stack([weight] * lax.axis_size('dp')), 'dp', 0, 0)]
where the time goes in v1:
time: 743 us
  waiting for transfers between devices  424 us (57%)
  blocking collectives  250 us (34%)
  matrix products  29.8 us (4%)
  between operations  16.5 us (2%)
  starting transfers between devices  11.9 us (2%)
    reduce_scatter x1, waiting for transfers between devices, on_device(): lax.psum_scatter(lax.dot_general(stacked, flat_grads, (((0,), (0,)), ((),...  183 us
    all_to_all x1, waiting for transfers between devices, on_device(): lax.all_to_all(jnp.stack([weight] * lax.axis_size('dp')), 'dp', 0, 0)  162 us
    psum x1, blocking collectives, on_device(): total_loss = lax.psum(local_share, ('dp', 'feat'))  77.6 us
    psum x1, blocking collectives, on_device(): col_sum = lax.psum(jnp.sum(views, axis=1), 'dp')  74.1 us
    psum x1, blocking collectives, on_device(): second_sum = lax.psum(jnp.sum(centered * centered, axis=1), 'dp')  72 us
    psum x1, waiting for transfers between devices, on_device(): lax.psum(gram_part.astype(jnp.bfloat16), 'feat').astype(jnp.float32)  59.9 us
    all_gather x1, waiting for transfers between devices, on_device(): gathered = lax.all_gather(centered_half, 'dp', axis=1, tiled=True)  19.7 us
  transfers between devices with their start and end apart: 5, of which 4 were waited for; matrix products, arithmetic and copies ran while one was open for 1% of the time, Pallas kernels for 0%

profile of v1, /device:TPU:8, one launch (start us, length us, event | category | flops | bytes accessed | tf_op | source)
XLA Modules:
  0.0 742.5 jit_solution(17096508511477184984)
XLA Ops:
  7.2 5.2 stack.4
  12.4 11.6 %all-to-all-start = ((bf16[32,128,1024]{2,1,0:T(8,128)(2,1)}), bf16[32,128,1024]{2,1,0:T(8,128)(2,1)}, u32[]{:S(2)}, u32[]{:S(2)}) async-start(bf16[32,128,1024]{2,1,0:T(8,128)(2,1)} %stack.4), calls=%async_computation | async-start | bytes 16777216 | tf_op jit(solution)/shard_map/all_to_all | solution.py:20
  24.0 13.3 %all_gather.9 = bf16[64,4096]{1,0:T(8,128)(2,1)S(1)} all-gather(bf16[64,512]{1,0:T(8,128)(2,1)S(1)} %copy-done.1), channel_id=1, replica_groups=mesh['dp'=32,'feat'=8] {'feat'}, dimensions={1}, use_global_device_ids=true | all-gather | bytes 589824 | tf_op jit(solution)/shard_map/all_gather | solution.py:15
  37.4 13.1 %all_gather.10 = bf16[64,4096]{1,0:T(8,128)(2,1)S(1)} all-gather(bf16[64,512]{1,0:T(8,128)(2,1)S(1)} %copy-done.2), channel_id=1, replica_groups=mesh['dp'=32,'feat'=8] {'feat'}, dimensions={1}, use_global_device_ids=true | all-gather | bytes 589824 | tf_op jit(solution)/shard_map/all_gather | solution.py:16
  50.6 162.2 %all-to-all-done = bf16[32,128,1024]{2,1,0:T(8,128)(2,1)} async-done(((bf16[32,128,1024]{2,1,0:T(8,128)(2,1)}), bf16[32,128,1024]{2,1,0:T(8,128)(2,1)}, u32[]{:S(2)}, u32[]{:S(2)}) %all-to-all-start) | async-done | bytes 8388640 | tf_op jit(solution)/shard_map/all_to_all | solution.py:20
  212.8 4.6 bitcast_reduce_fusion
  217.4 74.1 %psum.28 = f32[2,1024]{1,0:T(2,128)S(1)} all-reduce(f32[2,1024]{1,0:T(2,128)S(1)} %get-tuple-element.15), channel_id=1, replica_groups=mesh['dp'=32,'feat'=8] {'dp'}, use_global_device_ids=true, to_apply=%region_2.0 | all-reduce | flops 2048 | bytes 16384 | tf_op jit(solution)/shard_map/psum | solution.py:24
  291.5 0.8 fusion.5
  292.3 0.0 all-reduce.2.cloned.1.call-start
  292.4 72.0 %psum.29 = f32[2,1024]{1,0:T(2,128)S(1)} all-reduce(f32[2,1024]{1,0:T(2,128)S(1)} %get-tuple-element.7), channel_id=1, replica_groups=mesh['dp'=32,'feat'=8] {'dp'}, use_global_device_ids=true, to_apply=%region_4.0 | all-reduce | flops 2048 | bytes 16384 | tf_op jit(solution)/shard_map/psum | solution.py:27
  364.4 19.7 %all-gather.2.cloned.1.call-done = bf16[2,2048,1024]{2,1,0:T(8,128)(2,1)} async-done(((bf16[2,64,1024]{2,1,0:T(8,128)(2,1)}), bf16[2,2048,1024]{2,1,0:T(8,128)(2,1)}) %all-gather.2.cloned.1.call-update) | async-done | bytes 8388624 | tf_op jit(solution)/shard_map/all_gather | solution.py:31
  384.1 6.9 convolution_convert_fusion.2
  391.0 0.0 reduce-scatter.5.cloned.1.call-start
  391.1 0.6 multiply_reduce_fusion.3
  391.7 0.7 fusion.8
  392.4 59.9 %all-reduce.2.cloned.1.call-done = bf16[2,64,2048]{2,1,0:T(8,128)(2,1)} async-done(((bf16[2,64,2048]{2,1,0:T(8,128)(2,1)}), bf16[2,64,2048]{2,1,0:T(8,128)(2,1)}) %all-reduce.2.cloned.1.call-update) | async-done | bytes 524304 | tf_op jit(solution)/shard_map/psum | solution.py:35
  452.3 5.3 fusion.3
  457.6 7.3 convolution_convert_fusion.1
  465.0 0.2 reduce-scatter.3.cloned.1.call-start
  465.2 5.6 convolution_convert_fusion
  472.8 0.9 multiply_reduce_fusion
  474.3 77.6 %psum.31 = f32[]{:T(128)} all-reduce(f32[]{:T(128)S(6)} %add.33), channel_id=1, replica_groups=mesh['dp'=32,'feat'=8] {'dp','feat'}, use_global_device_ids=true, to_apply=%region_9.10 | all-reduce | flops 1 | bytes 8 | tf_op jit(solution)/shard_map/psum | solution.py:48
  551.9 1.5 fusion.9
  553.4 182.6 %reduce-scatter.3.cloned.1.call-done = bf16[128,1024]{1,0:T(8,128)(2,1)} async-done(((bf16[4096,1024]{1,0:T(8,128)(2,1)}), bf16[128,1024]{1,0:T(8,128)(2,1)}) %reduce-scatter.3.cloned.1.call-update) | async-done | bytes 262160 | tf_op jit(solution)/shard_map/reduce_scatter | solution.py:72
  (15 shorter events, 0.2 us)
Async XLA Ops:
  12.4 11.6 %copy-start.1 = (bf16[64,512]{1,0:T(8,128)(2,1)S(1)}, bf16[64,512]{1,0:T(8,128)(2,1)}, u32[]{:S(2)}) copy-start(bf16[64,512]{1,0:T(8,128)(2,1)} %param.3) | copy-start | bytes 196612
  12.4 25.0 %copy-start.2 = (bf16[64,512]{1,0:T(8,128)(2,1)S(1)}, bf16[64,512]{1,0:T(8,128)(2,1)}, u32[]{:S(2)}) copy-start(bf16[64,512]{1,0:T(8,128)(2,1)} %param.4) | copy-start | bytes 196612
  12.4 200.4 %all-to-all-start = ((bf16[32,128,1024]{2,1,0:T(8,128)(2,1)}), bf16[32,128,1024]{2,1,0:T(8,128)(2,1)}, u32[]{:S(2)}, u32[]{:S(2)}) async-start(bf16[32,128,1024]{2,1,0:T(8,128)(2,1)} %stack.4), calls=%async_computation | async-start | bytes 16777216 | tf_op jit(solution)/shard_map/all_to_all | solution.py:20
  24.0 360.1 %all-gather.2.cloned.1.call-start = ((), (), s32[]{:S(2)}) async-start(), calls=%async_computation.3 | async-start | bytes 8650752 | tf_op jit(solution)/shard_map/all_gather | solution.py:31
  292.3 160.0 %all-reduce.2.cloned.1.call-start = ((), (), s32[]{:S(2)}) async-start(), calls=%async_computation.4 | async-start | bytes 1048576 | tf_op jit(solution)/shard_map/psum | solution.py:35
  391.0 160.8 %reduce-scatter.5.cloned.1.call-start = ((), (), s32[]{:S(2)}) async-start(), calls=%async_computation.6 | async-start | bytes 1179648 | tf_op jit(solution)/shard_map/reduce_scatter | solution.py:67
  465.0 7.8 %copy-start = (bf16[2,64,2048]{2,1,0:T(8,128)(2,1)S(1)}, bf16[2,64,2048]{2,1,0:T(8,128)(2,1)}, u32[]{:S(2)}) copy-start(bf16[2,64,2048]{2,1,0:T(8,128)(2,1)} %all-reduce.2.cloned.1.call-done) | copy-start | bytes 1572868
  465.0 271.0 %reduce-scatter.3.cloned.1.call-start = ((), (), s32[]{:S(2)}) async-start(), calls=%async_computation.5 | async-start | bytes 8650752 | tf_op jit(solution)/shard_map/reduce_scatter | solution.py:72
Sparse Core Ops, SparseCore 0:
  292.4 91.5 all-gather.1
  391.2 61.1 all-reduce.1
  465.1 33.3 reduce-scatter.4
  502.9 233.0 reduce-scatter.2
